TPU v7x, 128 devices: a whole 4x4x4 slice. The times are simulated.
128 devices in a mesh: row: 16 (over z_hi, y, core), col: 8 (over z_lo, x).
Axes of the slice: x: 4, y: 4, z: 4 (z_hi: 2, z_lo: 2; z = z_hi * 2 + z_lo), core: 2. Of those that a mesh axis runs over, the one named last changes fastest.
Arguments:
- multispectral: bfloat16 [2, 32768, 4096], P(None, 'row', 'col'), may hold values from -6 to 6
- hyperspectral: bfloat16 [96, 8192, 1024], P(None, 'row', 'col'), may hold values from -6 to 6
- row_start: float32 [32768, 128], P(('row', 'col')), may hold values from -6 to 6
- col_factor: bfloat16 [4096, 128], P('col', 'row'), may hold values from -0.09375 to 0.09375
- band_factor: float32 [96, 128], replicated, may hold values from -2 to 2
- response: float32 [2, 96], replicated, may hold values from 0.2 to 1
- blur_taps: float32 [9], replicated, may hold values from 0.2 to 1
- offsets: int32 [9], replicated, may hold values from -8 to 8, as said below
Outputs:
- row_factor: float32 [32768, 128], P(('row', 'col'))
- residual: float32 [32768, 128], P(('row', 'col'))
Inputs may be any that keep to these rules, and one draw needn't show every extreme that they name: 9 distinct offsets; -8 and 8 are always among them.
All inputs are finite; a program needn't handle non-finite values.
Results may differ from a plain program's by a relative error of at most 0.0023.
Values may be sent and summed in bfloat16 or wider, within the bound.
A program may use at most 128 MiB of HBM per device.

v0:
```python
import jax
import jax.numpy as jnp
from jax import lax
from jax.sharding import PartitionSpec as P

DEC = 4
W = 8
ITERS = 4
RIDGE_TERM = 0.1
FULL_PRECISION = lax.Precision.HIGHEST


def extended(cells, sides, width):
    for axis, dim in sides:
        count = lax.axis_size(axis)
        head = lax.slice_in_dim(cells, 0, width, axis=dim)
        tail = lax.slice_in_dim(cells, cells.shape[dim] - width, cells.shape[dim], axis=dim)
        cells = jnp.concatenate(
            [
                lax.ppermute(tail, axis, [(i, (i + 1) % count) for i in range(count)]),
                cells,
                lax.ppermute(head, axis, [((i + 1) % count, i) for i in range(count)]),
            ],
            axis=dim,
        )
    return cells


def tap_places(offsets):
    reach = offsets + W
    return (reach // DEC, reach % DEC)


def blur_down(wide, weights, offsets, rows_out):
    shifts, phases = tap_places(offsets)
    quads = wide.reshape(wide.shape[0] // DEC, DEC, wide.shape[1])
    total = jnp.zeros((rows_out, wide.shape[1]), jnp.float32)
    for number in range(weights.shape[0]):
        piece = lax.dynamic_slice(
            quads, (shifts[number], phases[number], 0), (rows_out, 1, wide.shape[1])
        )[:, 0, :]
        total = total + weights[number] * piece.astype(jnp.float32)
    return total


def blur_up(coarse_wide, weights, offsets, margin):
    shifts, phases = tap_places(offsets)
    rows = coarse_wide.shape[0] - 2 * margin
    columns = coarse_wide.shape[1]
    parts = [jnp.zeros((rows, columns), jnp.float32) for _ in range(DEC)]
    for number in range(weights.shape[0]):
        piece = lax.dynamic_slice_in_dim(coarse_wide, margin + 2 - shifts[number], rows, 0)
        for phase in range(DEC):
            scale = jnp.where(phases[number] == phase, weights[number], jnp.float32(0.0))
            parts[phase] = parts[phase] + scale * piece
    return jnp.stack(parts, axis=1).reshape(rows * DEC, columns)


def body(
    multispectral, hyperspectral, row_start, col_factor, band_factor, response, blur_taps, offsets
):
    low_reach = (W + DEC - 1) // DEC
    columns = lax.all_gather(col_factor, "row", axis=1, tiled=True)
    column_wide = extended(columns, (("col", 0),), W)
    coarse_columns = blur_down(column_wide, blur_taps, offsets, columns.shape[0] // DEC)
    merged = jnp.dot(response, band_factor, precision=FULL_PRECISION)
    multi_pairs = (merged[:, None, :] * columns.astype(jnp.float32)[None, :, :]).astype(
        jnp.bfloat16
    )
    hyper_pairs = (band_factor[:, None, :] * coarse_columns[None, :, :]).astype(jnp.bfloat16)
    multi_part = jnp.einsum(
        "kij,kjr->ir", multispectral, multi_pairs, preferred_element_type=jnp.float32
    )
    hyper_part = jnp.einsum(
        "kij,kjr->ir", hyperspectral, hyper_pairs, preferred_element_type=jnp.float32
    )
    column_part = jnp.einsum("jr,js->rs", columns, columns, preferred_element_type=jnp.float32)
    coarse_part = jnp.einsum("jr,js->rs", coarse_columns, coarse_columns, precision=FULL_PRECISION)
    column_gram, coarse_gram = lax.psum((column_part, coarse_part), "col")
    band_gram = jnp.dot(band_factor.T, band_factor, precision=FULL_PRECISION)
    merged_gram = jnp.dot(merged.T, merged, precision=FULL_PRECISION)
    hyper_gram = coarse_gram * band_gram
    multi_gram = column_gram * merged_gram
    multi_sums, hyper_sums = lax.psum((multi_part, hyper_part), "col")
    start_rows = lax.all_gather(row_start, "col", axis=0, tiled=True)

    def inner_sum(first_field, second_field):
        return lax.psum(jnp.sum(first_field * second_field), "row")

    fine_rows = start_rows.shape[0]
    coarse_rows = fine_rows // DEC
    fine_reach = W + DEC * low_reach

    def operate(values):
        fine_wide = extended(values, (("row", 0),), fine_reach)
        coarse_wide = blur_down(fine_wide, blur_taps, offsets, coarse_rows + 2 * low_reach)
        restored = blur_up(coarse_wide, blur_taps, offsets, low_reach)
        return (
            jnp.dot(restored, hyper_gram, precision=FULL_PRECISION)
            + jnp.dot(values, multi_gram, precision=FULL_PRECISION)
            + RIDGE_TERM * values
        )

    hyper_wide = extended(hyper_sums, (("row", 0),), low_reach)
    right_side = blur_up(hyper_wide, blur_taps, offsets, low_reach) + multi_sums
    solution = start_rows
    residual = right_side - operate(solution)
    direction = residual
    norm_now = inner_sum(residual, residual)
    for iteration in range(ITERS):
        mapped = operate(direction)
        step_size = norm_now / inner_sum(direction, mapped)
        solution = solution + step_size * direction
        residual = residual - step_size * mapped
        norm_next = inner_sum(residual, residual)
        direction = residual + norm_next / norm_now * direction
        norm_now = norm_next
    portion = solution.shape[0] // lax.axis_size("col")
    corner = lax.axis_index("col") * portion
    solution = lax.dynamic_slice_in_dim(solution, corner, portion, 0)
    residual = lax.dynamic_slice_in_dim(residual, corner, portion, 0)
    return (solution, residual)


def solution(mesh):
    in_specs = (
        P(None, "row", "col"),
        P(None, "row", "col"),
        P(("row", "col"), None),
        P("col", "row"),
        P(),
        P(),
        P(),
        P(),
    )
    out_specs = (P(("row", "col"), None), P(("row", "col"), None))
    return jax.shard_map(body, mesh=mesh, in_specs=in_specs, out_specs=out_specs, check_vma=False)
```

profile of v0, /device:TPU:0, one launch (start us, length us, event | category | flops | bytes accessed | tf_op | source)
XLA Modules:
  0.0 637.7 jit_solution(14981827791086670884)
XLA Ops:
  7.2 25.9 %all_gather.7 = bf16[512,128]{0,1:T(8,128)(2,1)S(1)} all-gather(bf16[512,8]{0,1:T(8,128)(2,1)} %param.11), channel_id=1, replica_groups=mesh['row'=16,'col'=8] {'row'}, dimensions={1}, use_global_device_ids=true | all-gather | bytes 139264 | tf_op jit(solution)/shard_map/all_gather | solution.py:63
  33.3 1.6 collective-permute-start
  34.9 2.6 collective-permute-start.1
  56.8 4.7 convolution_bitcast_fusion.1
  80.9 5.6 add_bitcast_fusion.4
  87.5 8.2 %fusion.10 = f32[512,128]{0,1:T(8,128)} fusion(bf16[96,512,128]{2,1,0:T(8,128)(2,1)} %param.9, f32[128,128]{0,1:T(8,128)S(1)} %copy.270, f32[96,128]{1,0:T(8,128)S(1)} %copy-done.7), kind=kOutput, calls=%fused_computation.17 | convolution fusion | flops 1613758464 | bytes 12959744 | tf_op jit(solution)/shard_map/kij,kjr->ir/dot_general | solution.py:74
  164.5 5.0 all-reduce.4.cloned.1.call-done
  170.5 5.3 collective-permute-start.3
  182.1 28.2 %all-gather.2.cloned.1.call-done = f32[2048,128]{0,1:T(8,128)} async-done(((f32[256,128]{0,1:T(8,128)}), f32[2048,128]{0,1:T(8,128)}) %all-gather.2.cloned.1.call-update) | async-done | bytes 1048592 | tf_op jit(solution)/shard_map/all_gather | solution.py:85
  210.3 1.6 fusion.80
  211.9 5.5 collective-permute-start.5
  220.5 2.3 constant_dynamic-slice_fusion.43
  222.9 5.8 fusion.43
  233.7 5.6 collective-permute-start.7
  239.3 1.7 collective-permute-done.6
  242.3 2.3 constant_dynamic-slice_fusion.29
  244.6 5.8 fusion.35
  253.6 2.0 multiply_reduce_fusion.6
  255.5 39.2 %all-reduce = (f32[]{:T(128)}, f32[]{:T(128)}) all-reduce(f32[]{:T(128)} %get-tuple-element.11, f32[]{:T(128)} %get-tuple-element.10), channel_id=1, replica_groups=mesh['row'=16,'col'=8] {'row'}, use_global_device_ids=true, to_apply=%region_5.6 | all-reduce | flops 2 | bytes 16 | tf_op jit(solution)/shard_map/psum | solution.py:88
  296.9 33.8 %psum.90 = f32[]{:T(128)} all-reduce(f32[]{:T(128)} %multiply_reduce_fusion.5), channel_id=1, replica_groups=mesh['row'=16,'col'=8] {'row'}, use_global_device_ids=true, to_apply=%region_9.10 | all-reduce | flops 1 | bytes 8 | tf_op jit(solution)/shard_map/psum | solution.py:88
  332.3 5.6 collective-permute-start.9
  337.9 1.7 collective-permute-done.8
  341.2 2.6 copy.298
  343.8 7.2 %constant_dynamic-slice_fusion.17 = (f32[516,1,128]{2,1,0:T(1,128)S(1)}, f32[516,1,128]{2,1,0:T(1,128)S(1)}, f32[516,1,128]{2,1,0:T(1,128)S(1)}, f32[516,1,128]{...) fusion(f32[520,4,128]{2,1,0:T(4,128)} %bitcast.340, ...), kind=kLoop, calls=%fused_computation.222 | loop fusion | bytes 4755528 | tf_op jit(solution)/shard_map/dynamic_slice | solution.py:39
  351.0 5.8 fusion.27
  360.0 2.9 multiply_reduce_fusion.4
  362.8 39.2 %psum.91 = f32[]{:T(128)} all-reduce(f32[]{:T(128)} %get-tuple-element.120), channel_id=1, replica_groups=mesh['row'=16,'col'=8] {'row'}, use_global_device_ids=true, to_apply=%region_11.12 | all-reduce | flops 1 | bytes 8 | tf_op jit(solution)/shard_map/psum | solution.py:88
  403.3 3.0 multiply_reduce_fusion.3
  406.3 33.8 %psum.92 = f32[]{:T(128)} all-reduce(f32[]{:T(128)} %get-tuple-element.20), channel_id=1, replica_groups=mesh['row'=16,'col'=8] {'row'}, use_global_device_ids=true, to_apply=%region_13.14 | all-reduce | flops 1 | bytes 8 | tf_op jit(solution)/shard_map/psum | solution.py:88
  441.5 1.4 multiply_add_fusion.1
  443.0 5.8 collective-permute-start.11
  448.8 1.5 collective-permute-done.10
  452.0 2.6 copy.311
  454.6 7.2 %constant_dynamic-slice_fusion.8 = (f32[516,1,128]{2,1,0:T(1,128)S(1)}, f32[516,1,128]{2,1,0:T(1,128)S(1)}, f32[516,1,128]{2,1,0:T(1,128)S(1)}, f32[516,1,128]{2...) fusion(f32[520,4,128]{2,1,0:T(4,128)} %bitcast.341, ...), kind=kLoop, calls=%fused_computation.213 | loop fusion | bytes 4755528 | tf_op jit(solution)/shard_map/dynamic_slice | solution.py:39
  461.9 5.8 fusion.19
  470.8 2.8 multiply_reduce_fusion.2
  473.7 39.2 %psum.93 = f32[]{:T(128)} all-reduce(f32[]{:T(128)} %get-tuple-element.122), channel_id=1, replica_groups=mesh['row'=16,'col'=8] {'row'}, use_global_device_ids=true, to_apply=%region_15.16 | all-reduce | flops 1 | bytes 8 | tf_op jit(solution)/shard_map/psum | solution.py:88
  514.2 3.4 multiply_reduce_fusion.1
  517.6 33.8 %psum.94 = f32[]{:T(128)} all-reduce(f32[]{:T(128)} %get-tuple-element.18), channel_id=1, replica_groups=mesh['row'=16,'col'=8] {'row'}, use_global_device_ids=true, to_apply=%region_17.18 | all-reduce | flops 1 | bytes 8 | tf_op jit(solution)/shard_map/psum | solution.py:88
  552.8 1.4 multiply_add_fusion
  555.9 5.5 collective-permute-start.13
  561.4 2.0 collective-permute-done.12
  563.4 2.3 concatenate.27
  565.7 2.6 copy.324
  568.3 7.2 %constant_dynamic-slice_fusion.44 = (f32[516,1,128]{2,1,0:T(1,128)S(1)}, f32[516,1,128]{2,1,0:T(1,128)S(1)}, f32[516,1,128]{2,1,0:T(1,128)S(1)}, f32[516,1,128]{...) fusion(f32[520,4,128]{2,1,0:T(4,128)} %bitcast.337, ...), kind=kLoop, calls=%fused_computation.249 | loop fusion | bytes 4755528 | tf_op jit(solution)/shard_map/dynamic_slice | solution.py:39
  575.6 5.8 fusion.11
  584.7 2.8 multiply_reduce_fusion
  587.5 39.1 %psum.95 = f32[]{:T(128)} all-reduce(f32[]{:T(128)} %get-tuple-element.124), channel_id=1, replica_groups=mesh['row'=16,'col'=8] {'row'}, use_global_device_ids=true, to_apply=%region_19.20 | all-reduce | flops 1 | bytes 8 | tf_op jit(solution)/shard_map/psum | solution.py:88
  (117 shorter events, 46.0 us)
Async XLA Ops:
  7.2 49.5 %copy-start = (f32[2,96]{1,0:T(2,128)S(1)}, f32[2,96]{1,0:T(2,128)}, u32[]{:S(2)}) copy-start(f32[2,96]{1,0:T(2,128)} %param.13) | copy-start | bytes 2308
  7.2 48.8 %copy-start.9 = (f32[9]{0:T(128)S(1)}, f32[9]{0:T(128)}, u32[]{:S(2)}) copy-start(f32[9]{0:T(128)} %param.14) | copy-start | bytes 112
  7.2 49.5 %copy-start.7 = (f32[96,128]{1,0:T(8,128)S(1)}, f32[96,128]{1,0:T(8,128)}, u32[]{:S(2)}) copy-start(f32[96,128]{1,0:T(8,128)} %param.12) | copy-start | bytes 147460
  7.2 162.3 %all-reduce.4.cloned.1.call-start = ((), (), s32[]{:S(2)}) async-start(), calls=%async_computation.1 | async-start | bytes 2883584 | tf_op jit(solution)/shard_map/psum | solution.py:79
  33.3 46.9 %collective-permute-start = (bf16[8,128]{1,0:T(8,128)(2,1)S(1)}, bf16[8,128]{1,0:T(8,128)(2,1)S(1)}, u32[]{:S(2)}, u32[]{:S(2)}) collective-permute-start(bf16[8,128]{1,0:T(8,128)(2,1)S(1)} %get-tuple-element.90), channel_id=1, source_target_pairs={{0,1},{1,2},{2,3},{3,4},{4,5},{5,6},{6,7},{7,0},{8,9},{9,10},{10,1... | collective-permute-start | bytes 6152 | tf_op jit(solution)/shard_map/ppermute | solution.py:20
  34.9 45.3 %collective-permute-start.1 = (bf16[8,128]{1,0:T(8,128)(2,1)S(1)}, bf16[8,128]{1,0:T(8,128)(2,1)S(1)}, u32[]{:S(2)}, u32[]{:S(2)}) collective-permute-start(bf16[8,128]{1,0:T(8,128)(2,1)S(1)} %get-tuple-element.91), channel_id=1, source_target_pairs={{1,0},{2,1},{3,2},{4,3},{5,4},{6,5},{7,6},{0,7},{9,8},{10,9},{11,1... | collective-permute-start | bytes 6152 | tf_op jit(solution)/shard_map/ppermute | solution.py:22
  95.7 0.9 copy-start.8
  95.7 114.6 %all-gather.2.cloned.1.call-start = ((), (), s32[]{:S(2)}) async-start(), calls=%async_computation | async-start | bytes 1179648 | tf_op jit(solution)/shard_map/all_gather | solution.py:85
  170.5 7.7 %collective-permute-start.2 = (f32[2,128]{0,1:T(8,128)S(1)}, f32[2,128]{0,1:T(8,128)S(1)}, u32[]{:S(2)}, u32[]{:S(2)}) collective-permute-start(f32[2,128]{0,1:T(8,128)S(1)} %get-tuple-element.79), channel_id=1, source_target_pairs={{0,8},{8,16},{16,24},{24,32},{32,40},{40,48},{48,56},{56,64},{64,7... | collective-permute-start | bytes 3080 | tf_op jit(solution)/shard_map/ppermute | solution.py:20
  170.5 7.6 %collective-permute-start.3 = (f32[2,128]{0,1:T(8,128)S(1)}, f32[2,128]{0,1:T(8,128)S(1)}, u32[]{:S(2)}, u32[]{:S(2)}) collective-permute-start(f32[2,128]{0,1:T(8,128)S(1)} %get-tuple-element.80), channel_id=1, source_target_pairs={{8,0},{16,8},{24,16},{32,24},{40,32},{48,40},{56,48},{64,56},{72,6... | collective-permute-start | bytes 3080 | tf_op jit(solution)/shard_map/ppermute | solution.py:22
  211.9 7.5 %collective-permute-start.4 = (f32[16,128]{0,1:T(8,128)}, f32[16,128]{0,1:T(8,128)S(1)}, u32[]{:S(2)}, u32[]{:S(2)}) collective-permute-start(f32[16,128]{0,1:T(8,128)} %get-tuple-element.78), channel_id=1, source_target_pairs={{0,8},{8,16},{16,24},{24,32},{32,40},{40,48},{48,56},{56,64},{64,7... | collective-permute-start | bytes 24584 | tf_op jit(solution)/shard_map/ppermute | solution.py:20
  211.9 7.5 %collective-permute-start.5 = (f32[16,128]{0,1:T(8,128)S(1)}, f32[16,128]{0,1:T(8,128)S(1)}, u32[]{:S(2)}, u32[]{:S(2)}) collective-permute-start(f32[16,128]{0,1:T(8,128)S(1)} %get-tuple-element.77), channel_id=1, source_target_pairs={{8,0},{16,8},{24,16},{32,24},{40,32},{48,40},{56,48},{64,56},{72,6... | collective-permute-start | bytes 24584 | tf_op jit(solution)/shard_map/ppermute | solution.py:22
  217.9 1.6 copy-start.4
  230.7 1.2 copy-start.5
  230.7 1.5 copy-start.6
  233.6 7.3 %collective-permute-start.6 = (f32[16,128]{0,1:T(8,128)S(1)}, f32[16,128]{0,1:T(8,128)S(1)}, u32[]{:S(2)}, u32[]{:S(2)}) collective-permute-start(f32[16,128]{0,1:T(8,128)S(1)} %get-tuple-element.76), channel_id=1, source_target_pairs={{0,8},{8,16},{16,24},{24,32},{32,40},{40,48},{48,56},{56,64},{64,7... | collective-permute-start | bytes 24584 | tf_op jit(solution)/shard_map/ppermute | solution.py:20
  233.7 7.5 %collective-permute-start.7 = (f32[16,128]{0,1:T(8,128)S(1)}, f32[16,128]{0,1:T(8,128)S(1)}, u32[]{:S(2)}, u32[]{:S(2)}) collective-permute-start(f32[16,128]{0,1:T(8,128)S(1)} %get-tuple-element.75), channel_id=1, source_target_pairs={{8,0},{16,8},{24,16},{32,24},{40,32},{48,40},{56,48},{64,56},{72,6... | collective-permute-start | bytes 24584 | tf_op jit(solution)/shard_map/ppermute | solution.py:22
  332.3 7.3 %collective-permute-start.8 = (f32[16,128]{0,1:T(8,128)S(1)}, f32[16,128]{0,1:T(8,128)S(1)}, u32[]{:S(2)}, u32[]{:S(2)}) collective-permute-start(f32[16,128]{0,1:T(8,128)S(1)} %get-tuple-element.74), channel_id=1, source_target_pairs={{0,8},{8,16},{16,24},{24,32},{32,40},{40,48},{48,56},{56,64},{64,7... | collective-permute-start | bytes 24584 | tf_op jit(solution)/shard_map/ppermute | solution.py:20
  332.3 7.5 %collective-permute-start.9 = (f32[16,128]{0,1:T(8,128)S(1)}, f32[16,128]{0,1:T(8,128)S(1)}, u32[]{:S(2)}, u32[]{:S(2)}) collective-permute-start(f32[16,128]{0,1:T(8,128)S(1)} %get-tuple-element.73), channel_id=1, source_target_pairs={{8,0},{16,8},{24,16},{32,24},{40,32},{48,40},{56,48},{64,56},{72,6... | collective-permute-start | bytes 24584 | tf_op jit(solution)/shard_map/ppermute | solution.py:22
  443.0 7.3 %collective-permute-start.10 = (f32[16,128]{0,1:T(8,128)S(1)}, f32[16,128]{0,1:T(8,128)S(1)}, u32[]{:S(2)}, u32[]{:S(2)}) collective-permute-start(f32[16,128]{0,1:T(8,128)S(1)} %get-tuple-element.72), channel_id=1, source_target_pairs={{0,8},{8,16},{16,24},{24,32},{32,40},{40,48},{48,56},{56,64},{64,7... | collective-permute-start | bytes 24584 | tf_op jit(solution)/shard_map/ppermute | solution.py:20
  443.0 7.7 %collective-permute-start.11 = (f32[16,128]{0,1:T(8,128)S(1)}, f32[16,128]{0,1:T(8,128)S(1)}, u32[]{:S(2)}, u32[]{:S(2)}) collective-permute-start(f32[16,128]{0,1:T(8,128)S(1)} %get-tuple-element.71), channel_id=1, source_target_pairs={{8,0},{16,8},{24,16},{32,24},{40,32},{48,40},{56,48},{64,56},{72,6... | collective-permute-start | bytes 24584 | tf_op jit(solution)/shard_map/ppermute | solution.py:22
  554.2 1.0 copy-start.2
  555.9 7.5 %collective-permute-start.12 = (f32[16,128]{0,1:T(8,128)}, f32[16,128]{0,1:T(8,128)S(1)}, u32[]{:S(2)}, u32[]{:S(2)}) collective-permute-start(f32[16,128]{0,1:T(8,128)} %get-tuple-element.70), channel_id=1, source_target_pairs={{0,8},{8,16},{16,24},{24,32},{32,40},{40,48},{48,56},{56,64},{64,7... | collective-permute-start | bytes 24584 | tf_op jit(solution)/shard_map/ppermute | solution.py:20
  555.9 7.5 %collective-permute-start.13 = (f32[16,128]{0,1:T(8,128)S(1)}, f32[16,128]{0,1:T(8,128)S(1)}, u32[]{:S(2)}, u32[]{:S(2)}) collective-permute-start(f32[16,128]{0,1:T(8,128)S(1)} %get-tuple-element.69), channel_id=1, source_target_pairs={{8,0},{16,8},{24,16},{32,24},{40,32},{48,40},{56,48},{64,56},{72,6... | collective-permute-start | bytes 24584 | tf_op jit(solution)/shard_map/ppermute | solution.py:22
  583.4 1.2 copy-start.3
  584.7 46.0 %copy-start.1 = (f32[2,96]{1,0:T(2,128)S(1)}, f32[2,96]{1,0:T(2,128)}, u32[]{:S(2)}) copy-start(f32[2,96]{1,0:T(2,128)} %param.13) | copy-start | bytes 2308
Sparse Core Ops, SparseCore 0:
  95.8 73.6 all-reduce.3
  171.7 38.5 all-gather.1
where the time goes:
time: 648 us; the launch traced here: 638 us
  blocking collectives  284 us (44%)
  between operations  125 us (19%)
  other arithmetic  58.2 us (9%)
  local copies, waits for them, and re-layouts  57.5 us (9%)
  waiting for transfers between devices  41.1 us (6%)
  starting transfers between devices  37.8 us (6%)
  matrix products  34.2 us (5%)
    psum x7, blocking collectives, inner_sum(): return lax.psum(jnp.sum(first_field * second_field), 'row')  258 us
    ppermute x7, starting transfers between devices, extended(): lax.ppermute(head, axis, [((i + 1) % count, i) for i in range(count)])  36 us
    add x6, other arithmetic, blur_down(): total = total + weights[number] * piece.astype(jnp.float32)  34.5 us
    all_gather x1, waiting for transfers between devices, body(): start_rows = lax.all_gather(row_start, 'col', axis=0, tiled=True)  28.2 us
    dynamic_slice x6, local copies, waits for them, and re-layouts, blur_down(): lax.dynamic_slice(quads, (shifts[number], phases[number], 0), (rows_out,...  27 us
    all_gather x1, blocking collectives, body(): columns = lax.all_gather(col_factor, 'row', axis=1, tiled=True)  25.9 us
    concatenate x10, local copies, waits for them, and re-layouts, extended(): jnp.concatenate([lax.ppermute(tail, axis, [(i, (i + 1) % count) for i in...  14.9 us
  transfers between devices with their start and end apart: 16, of which 10 were waited for; matrix products, arithmetic and copies ran while one was open for 3% of the time, Pallas kernels for 0%

commit v1 on v0

--- a/solution.py
+++ b/solution.py
@@ -82,7 +82,8 @@
     hyper_gram = coarse_gram * band_gram
     multi_gram = column_gram * merged_gram
     multi_sums, hyper_sums = lax.psum((multi_part, hyper_part), "col")
-    start_rows = lax.all_gather(row_start, "col", axis=0, tiled=True)
+    stack = jnp.stack([row_start] * lax.axis_size("col"))
+    start_rows = jnp.concatenate(lax.all_to_all(stack, "col", 0, 0), axis=0)
 
     def inner_sum(first_field, second_field):
         return lax.psum(jnp.sum(first_field * second_field), "row")

time: 648 us -> 618 us (0.954)
  waiting for transfers between devices: 41.1 us -> 7.7 us
    all_gather x1 -> x0, waiting for transfers between devices: 28.2 us -> none  [body(): start_rows = lax.all_gather(row_start, 'col', axis=0, tiled=True)]
  transfers between devices with their start and end apart: 16 -> 16, of which waited for: 10 -> 7; matrix products, arithmetic and copies ran while one was open for 3% -> 7% of each run, Pallas kernels for 0% -> 0%
where the time goes in v1:
time: 618 us; the launch traced here: 607 us
  blocking collectives  284 us (46%)
  between operations  125 us (20%)
  local copies, waits for them, and re-layouts  56.1 us (9%)
  other arithmetic  56.1 us (9%)
  starting transfers between devices  41.4 us (7%)
  matrix products  36.2 us (6%)
  waiting for transfers between devices  7.7 us (1%)
    psum x7, blocking collectives, inner_sum(): return lax.psum(jnp.sum(first_field * second_field), 'row')  258 us
    ppermute x7, starting transfers between devices, extended(): lax.ppermute(head, axis, [((i + 1) % count, i) for i in range(count)])  35.9 us
    add x6, other arithmetic, blur_down(): total = total + weights[number] * piece.astype(jnp.float32)  34.6 us
    dynamic_slice x6, local copies, waits for them, and re-layouts, blur_down(): lax.dynamic_slice(quads, (shifts[number], phases[number], 0), (rows_out,...  27 us
    all_gather x1, blocking collectives, body(): columns = lax.all_gather(col_factor, 'row', axis=1, tiled=True)  25.9 us
    concatenate x10, local copies, waits for them, and re-layouts, extended(): jnp.concatenate([lax.ppermute(tail, axis, [(i, (i + 1) % count) for i in...  15 us
    dot_general x5, matrix products, operate(): jnp.dot(values, multi_gram, precision=FULL_PRECISION)  13.7 us
  transfers between devices with their start and end apart: 16, of which 7 were waited for; matrix products, arithmetic and copies ran while one was open for 7% of the time, Pallas kernels for 0%

profile of v1, /device:TPU:0, one launch (start us, length us, event | category | flops | bytes accessed | tf_op | source)
XLA Modules:
  0.0 606.7 jit_solution(4827874159508360752)
XLA Ops:
  7.2 25.9 %all_gather.3 = bf16[512,128]{0,1:T(8,128)(2,1)S(1)} all-gather(bf16[512,8]{0,1:T(8,128)(2,1)} %param.11), channel_id=1, replica_groups=mesh['row'=16,'col'=8] {'row'}, dimensions={1}, use_global_device_ids=true | all-gather | bytes 139264 | tf_op jit(solution)/shard_map/all_gather | solution.py:63
  33.2 1.6 collective-permute-start
  34.8 2.6 collective-permute-start.1
  39.5 3.7 all-to-all-start
  61.5 4.7 convolution_bitcast_fusion.1
  85.4 5.7 add_bitcast_fusion.4
  92.1 8.2 %fusion.10 = f32[512,128]{0,1:T(8,128)} fusion(bf16[96,512,128]{2,1,0:T(8,128)(2,1)} %param.9, f32[128,128]{0,1:T(8,128)S(1)} %copy.272, f32[96,128]{1,0:T(8,128)S(1)} %copy-done.6), kind=kOutput, calls=%fused_computation.17 | convolution fusion | flops 1613758464 | bytes 12959744 | tf_op jit(solution)/shard_map/kij,kjr->ir/dot_general | solution.py:74
  100.6 5.3 collective-permute-start.5
  174.3 2.3 constant_dynamic-slice_fusion.43
  176.7 5.8 fusion.43
  185.6 5.5 collective-permute-start.3
  192.3 2.1 fusion.88
  199.5 3.1 fusion.5
  202.8 5.7 collective-permute-start.7
  208.5 1.6 collective-permute-done.6
  211.5 2.3 constant_dynamic-slice_fusion.29
  213.9 5.8 fusion.35
  222.8 2.0 multiply_reduce_fusion.6
  224.8 39.2 %all-reduce = (f32[]{:T(128)}, f32[]{:T(128)}) all-reduce(f32[]{:T(128)} %get-tuple-element.11, f32[]{:T(128)} %get-tuple-element.10), channel_id=1, replica_groups=mesh['row'=16,'col'=8] {'row'}, use_global_device_ids=true, to_apply=%region_5.6 | all-reduce | flops 2 | bytes 16 | tf_op jit(solution)/shard_map/psum | solution.py:89
  266.2 33.8 %psum.90 = f32[]{:T(128)} all-reduce(f32[]{:T(128)} %multiply_reduce_fusion.5), channel_id=1, replica_groups=mesh['row'=16,'col'=8] {'row'}, use_global_device_ids=true, to_apply=%region_9.10 | all-reduce | flops 1 | bytes 8 | tf_op jit(solution)/shard_map/psum | solution.py:89
  301.6 5.5 collective-permute-start.9
  307.1 1.8 collective-permute-done.8
  310.4 2.6 copy.300
  313.0 7.2 %constant_dynamic-slice_fusion.17 = (f32[516,1,128]{2,1,0:T(1,128)S(1)}, f32[516,1,128]{2,1,0:T(1,128)S(1)}, f32[516,1,128]{2,1,0:T(1,128)S(1)}, f32[516,1,128]{...) fusion(f32[520,4,128]{2,1,0:T(4,128)} %bitcast.342, ...), kind=kLoop, calls=%fused_computation.222 | loop fusion | bytes 4755528 | tf_op jit(solution)/shard_map/dynamic_slice | solution.py:39
  320.2 5.8 fusion.27
  329.1 2.9 multiply_reduce_fusion.4
  332.0 39.2 %psum.91 = f32[]{:T(128)} all-reduce(f32[]{:T(128)} %get-tuple-element.120), channel_id=1, replica_groups=mesh['row'=16,'col'=8] {'row'}, use_global_device_ids=true, to_apply=%region_11.12 | all-reduce | flops 1 | bytes 8 | tf_op jit(solution)/shard_map/psum | solution.py:89
  372.5 3.0 multiply_reduce_fusion.3
  375.5 33.8 %psum.92 = f32[]{:T(128)} all-reduce(f32[]{:T(128)} %get-tuple-element.20), channel_id=1, replica_groups=mesh['row'=16,'col'=8] {'row'}, use_global_device_ids=true, to_apply=%region_13.14 | all-reduce | flops 1 | bytes 8 | tf_op jit(solution)/shard_map/psum | solution.py:89
  410.6 1.4 multiply_add_fusion.1
  412.2 5.5 collective-permute-start.11
  417.7 1.8 collective-permute-done.10
  421.0 2.6 copy.313
  423.6 7.2 %constant_dynamic-slice_fusion.8 = (f32[516,1,128]{2,1,0:T(1,128)S(1)}, f32[516,1,128]{2,1,0:T(1,128)S(1)}, f32[516,1,128]{2,1,0:T(1,128)S(1)}, f32[516,1,128]{2...) fusion(f32[520,4,128]{2,1,0:T(4,128)} %bitcast.343, ...), kind=kLoop, calls=%fused_computation.213 | loop fusion | bytes 4755528 | tf_op jit(solution)/shard_map/dynamic_slice | solution.py:39
  430.8 5.8 fusion.19
  439.7 2.8 multiply_reduce_fusion.2
  442.6 39.2 %psum.93 = f32[]{:T(128)} all-reduce(f32[]{:T(128)} %get-tuple-element.122), channel_id=1, replica_groups=mesh['row'=16,'col'=8] {'row'}, use_global_device_ids=true, to_apply=%region_15.16 | all-reduce | flops 1 | bytes 8 | tf_op jit(solution)/shard_map/psum | solution.py:89
  483.1 3.4 multiply_reduce_fusion.1
  486.5 33.8 %psum.94 = f32[]{:T(128)} all-reduce(f32[]{:T(128)} %get-tuple-element.18), channel_id=1, replica_groups=mesh['row'=16,'col'=8] {'row'}, use_global_device_ids=true, to_apply=%region_17.18 | all-reduce | flops 1 | bytes 8 | tf_op jit(solution)/shard_map/psum | solution.py:89
  521.6 1.4 multiply_add_fusion
  524.7 5.6 collective-permute-start.13
  530.3 1.9 collective-permute-done.12
  532.2 2.3 concatenate.27
  534.5 2.6 copy.326
  537.1 7.2 %constant_dynamic-slice_fusion.44 = (f32[516,1,128]{2,1,0:T(1,128)S(1)}, f32[516,1,128]{2,1,0:T(1,128)S(1)}, f32[516,1,128]{2,1,0:T(1,128)S(1)}, f32[516,1,128]{...) fusion(f32[520,4,128]{2,1,0:T(4,128)} %bitcast.339, ...), kind=kLoop, calls=%fused_computation.249 | loop fusion | bytes 4755528 | tf_op jit(solution)/shard_map/dynamic_slice | solution.py:39
  544.3 5.8 fusion.11
  553.4 2.8 multiply_reduce_fusion
  556.2 39.1 %psum.95 = f32[]{:T(128)} all-reduce(f32[]{:T(128)} %get-tuple-element.124), channel_id=1, replica_groups=mesh['row'=16,'col'=8] {'row'}, use_global_device_ids=true, to_apply=%region_19.20 | all-reduce | flops 1 | bytes 8 | tf_op jit(solution)/shard_map/psum | solution.py:89
  (118 shorter events, 40.5 us)
Async XLA Ops:
  7.2 54.2 %copy-start = (f32[2,96]{1,0:T(2,128)S(1)}, f32[2,96]{1,0:T(2,128)}, u32[]{:S(2)}) copy-start(f32[2,96]{1,0:T(2,128)} %param.13) | copy-start | bytes 2308
  33.2 51.4 %collective-permute-start = (bf16[8,128]{1,0:T(8,128)(2,1)S(1)}, bf16[8,128]{1,0:T(8,128)(2,1)S(1)}, u32[]{:S(2)}, u32[]{:S(2)}) collective-permute-start(bf16[8,128]{1,0:T(8,128)(2,1)S(1)} %get-tuple-element.90), channel_id=1, source_target_pairs={{0,1},{1,2},{2,3},{3,4},{4,5},{5,6},{6,7},{7,0},{8,9},{9,10},{10,1... | collective-permute-start | bytes 6152 | tf_op jit(solution)/shard_map/ppermute | solution.py:20
  34.8 49.9 %collective-permute-start.1 = (bf16[8,128]{1,0:T(8,128)(2,1)S(1)}, bf16[8,128]{1,0:T(8,128)(2,1)S(1)}, u32[]{:S(2)}, u32[]{:S(2)}) collective-permute-start(bf16[8,128]{1,0:T(8,128)(2,1)S(1)} %get-tuple-element.91), channel_id=1, source_target_pairs={{1,0},{2,1},{3,2},{4,3},{5,4},{6,5},{7,6},{0,7},{9,8},{10,9},{11,1... | collective-permute-start | bytes 6152 | tf_op jit(solution)/shard_map/ppermute | solution.py:22
  39.5 3.8 copy-start.9
  39.5 21.2 %copy-start.8 = (f32[9]{0:T(128)S(1)}, f32[9]{0:T(128)}, u32[]{:S(2)}) copy-start(f32[9]{0:T(128)} %param.14) | copy-start | bytes 112
  39.5 21.9 %copy-start.6 = (f32[96,128]{1,0:T(8,128)S(1)}, f32[96,128]{1,0:T(8,128)}, u32[]{:S(2)}) copy-start(f32[96,128]{1,0:T(8,128)} %param.12) | copy-start | bytes 147460
  39.5 60.8 %all-to-all-start = ((f32[8,256,128]{1,2,0:T(8,128)}), f32[8,256,128]{1,2,0:T(8,128)S(1)}, u32[]{:S(2)}, u32[]{:S(2)}) async-start(f32[8,256,128]{1,2,0:T(8,128)} %stack.101), calls=%async_computation | async-start | bytes 2097152 | tf_op jit(solution)/shard_map/all_to_all | solution.py:86
  43.2 141.4 %all-reduce.4.cloned.1.call-start = ((), (), s32[]{:S(2)}) async-start(), calls=%async_computation.1 | async-start | bytes 2883584 | tf_op jit(solution)/shard_map/psum | solution.py:79
  100.4 99.1 %copy-start.4 = (f32[8,16,8,256]{3,2,0,1:T(8,128)}, f32[8,16,8,256]{3,2,0,1:T(8,128)S(1)}, u32[]{:S(2)}) copy-start(f32[8,16,8,256]{3,2,0,1:T(8,128)S(1)} %copy.404) | copy-start | bytes 3145732
  100.5 72.7 %collective-permute-start.4 = (f32[16,128]{0,1:T(8,128)S(1)}, f32[16,128]{0,1:T(8,128)S(1)}, u32[]{:S(2)}, u32[]{:S(2)}) collective-permute-start(f32[16,128]{0,1:T(8,128)S(1)} %get-tuple-element.78), channel_id=1, source_target_pairs={{0,8},{8,16},{16,24},{24,32},{32,40},{40,48},{48,56},{56,64},{64,7... | collective-permute-start | bytes 24584 | tf_op jit(solution)/shard_map/ppermute | solution.py:20
  100.6 72.6 %collective-permute-start.5 = (f32[16,128]{0,1:T(8,128)S(1)}, f32[16,128]{0,1:T(8,128)S(1)}, u32[]{:S(2)}, u32[]{:S(2)}) collective-permute-start(f32[16,128]{0,1:T(8,128)S(1)} %get-tuple-element.77), channel_id=1, source_target_pairs={{8,0},{16,8},{24,16},{32,24},{40,32},{48,40},{56,48},{64,56},{72,6... | collective-permute-start | bytes 24584 | tf_op jit(solution)/shard_map/ppermute | solution.py:22
  185.5 9.1 %collective-permute-start.2 = (f32[2,128]{0,1:T(8,128)S(1)}, f32[2,128]{0,1:T(8,128)S(1)}, u32[]{:S(2)}, u32[]{:S(2)}) collective-permute-start(f32[2,128]{0,1:T(8,128)S(1)} %get-tuple-element.79), channel_id=1, source_target_pairs={{0,8},{8,16},{16,24},{24,32},{32,40},{40,48},{48,56},{56,64},{64,7... | collective-permute-start | bytes 3080 | tf_op jit(solution)/shard_map/ppermute | solution.py:20
  185.6 9.1 %collective-permute-start.3 = (f32[2,128]{0,1:T(8,128)S(1)}, f32[2,128]{0,1:T(8,128)S(1)}, u32[]{:S(2)}, u32[]{:S(2)}) collective-permute-start(f32[2,128]{0,1:T(8,128)S(1)} %get-tuple-element.80), channel_id=1, source_target_pairs={{8,0},{16,8},{24,16},{32,24},{40,32},{48,40},{56,48},{64,56},{72,6... | collective-permute-start | bytes 3080 | tf_op jit(solution)/shard_map/ppermute | solution.py:22
  192.3 2.1 copy-start.7
  192.3 2.4 copy-start.5
  202.7 7.3 %collective-permute-start.6 = (f32[16,128]{0,1:T(8,128)S(1)}, f32[16,128]{0,1:T(8,128)S(1)}, u32[]{:S(2)}, u32[]{:S(2)}) collective-permute-start(f32[16,128]{0,1:T(8,128)S(1)} %get-tuple-element.76), channel_id=1, source_target_pairs={{0,8},{8,16},{16,24},{24,32},{32,40},{40,48},{48,56},{56,64},{64,7... | collective-permute-start | bytes 24584 | tf_op jit(solution)/shard_map/ppermute | solution.py:20
  202.8 7.6 %collective-permute-start.7 = (f32[16,128]{0,1:T(8,128)S(1)}, f32[16,128]{0,1:T(8,128)S(1)}, u32[]{:S(2)}, u32[]{:S(2)}) collective-permute-start(f32[16,128]{0,1:T(8,128)S(1)} %get-tuple-element.75), channel_id=1, source_target_pairs={{8,0},{16,8},{24,16},{32,24},{40,32},{48,40},{56,48},{64,56},{72,6... | collective-permute-start | bytes 24584 | tf_op jit(solution)/shard_map/ppermute | solution.py:22
  301.6 7.3 %collective-permute-start.8 = (f32[16,128]{0,1:T(8,128)S(1)}, f32[16,128]{0,1:T(8,128)S(1)}, u32[]{:S(2)}, u32[]{:S(2)}) collective-permute-start(f32[16,128]{0,1:T(8,128)S(1)} %get-tuple-element.74), channel_id=1, source_target_pairs={{0,8},{8,16},{16,24},{24,32},{32,40},{40,48},{48,56},{56,64},{64,7... | collective-permute-start | bytes 24584 | tf_op jit(solution)/shard_map/ppermute | solution.py:20
  301.6 7.4 %collective-permute-start.9 = (f32[16,128]{0,1:T(8,128)S(1)}, f32[16,128]{0,1:T(8,128)S(1)}, u32[]{:S(2)}, u32[]{:S(2)}) collective-permute-start(f32[16,128]{0,1:T(8,128)S(1)} %get-tuple-element.73), channel_id=1, source_target_pairs={{8,0},{16,8},{24,16},{32,24},{40,32},{48,40},{56,48},{64,56},{72,6... | collective-permute-start | bytes 24584 | tf_op jit(solution)/shard_map/ppermute | solution.py:22
  412.1 7.3 %collective-permute-start.10 = (f32[16,128]{0,1:T(8,128)S(1)}, f32[16,128]{0,1:T(8,128)S(1)}, u32[]{:S(2)}, u32[]{:S(2)}) collective-permute-start(f32[16,128]{0,1:T(8,128)S(1)} %get-tuple-element.72), channel_id=1, source_target_pairs={{0,8},{8,16},{16,24},{24,32},{32,40},{40,48},{48,56},{56,64},{64,7... | collective-permute-start | bytes 24584 | tf_op jit(solution)/shard_map/ppermute | solution.py:20
  412.2 7.4 %collective-permute-start.11 = (f32[16,128]{0,1:T(8,128)S(1)}, f32[16,128]{0,1:T(8,128)S(1)}, u32[]{:S(2)}, u32[]{:S(2)}) collective-permute-start(f32[16,128]{0,1:T(8,128)S(1)} %get-tuple-element.71), channel_id=1, source_target_pairs={{8,0},{16,8},{24,16},{32,24},{40,32},{48,40},{56,48},{64,56},{72,6... | collective-permute-start | bytes 24584 | tf_op jit(solution)/shard_map/ppermute | solution.py:22
  523.0 1.0 copy-start.2
  524.7 7.5 %collective-permute-start.12 = (f32[16,128]{0,1:T(8,128)}, f32[16,128]{0,1:T(8,128)S(1)}, u32[]{:S(2)}, u32[]{:S(2)}) collective-permute-start(f32[16,128]{0,1:T(8,128)} %get-tuple-element.70), channel_id=1, source_target_pairs={{0,8},{8,16},{16,24},{24,32},{32,40},{40,48},{48,56},{56,64},{64,7... | collective-permute-start | bytes 24584 | tf_op jit(solution)/shard_map/ppermute | solution.py:20
  524.7 7.5 %collective-permute-start.13 = (f32[16,128]{0,1:T(8,128)S(1)}, f32[16,128]{0,1:T(8,128)S(1)}, u32[]{:S(2)}, u32[]{:S(2)}) collective-permute-start(f32[16,128]{0,1:T(8,128)S(1)} %get-tuple-element.69), channel_id=1, source_target_pairs={{8,0},{16,8},{24,16},{32,24},{40,32},{48,40},{56,48},{64,56},{72,6... | collective-permute-start | bytes 24584 | tf_op jit(solution)/shard_map/ppermute | solution.py:22
  552.2 1.2 copy-start.3
  553.4 46.0 %copy-start.1 = (f32[2,96]{1,0:T(2,128)S(1)}, f32[2,96]{1,0:T(2,128)}, u32[]{:S(2)}) copy-start(f32[2,96]{1,0:T(2,128)} %param.13) | copy-start | bytes 2308
Sparse Core Ops, SparseCore 0:
  100.4 76.6 all-reduce.3
